TPU v7x, 128 devices: a whole 4x4x4 slice. The times are simulated.
128 devices in a mesh: slab: 16 (over x, y_hi, core), tile: 8 (over y_lo, z).
Axes of the slice: x: 4, y: 4 (y_hi: 2, y_lo: 2; y = y_hi * 2 + y_lo), z: 4, core: 2. Of those that a mesh axis runs over, the one named last changes fastest.
Arguments:
- velocity: float32 [3, 512, 128, 128], P(None, 'slab', 'tile'), may hold values from -4 to 4
- viscosity: float32 [512, 128, 128], P('slab', 'tile'), may hold values from 0.2 to 0.6
- basis: bfloat16 [32, 3, 512, 128, 128], P(None, None, ('slab', 'tile')), may hold values from -6 to 6
- sigma: float32 [32], replicated, may hold values from 0.3 to 3
- rotation: float32 [35, 32], replicated, may hold values from -1 to 1
Outputs:
- advanced: float32 [3, 512, 128, 128], P(None, 'slab', 'tile')
- r_factor: float32 [35, 35], replicated
- new_basis: bfloat16 [32, 3, 512, 128, 128], P(None, None, ('slab', 'tile'))
All inputs are finite; a program needn't handle non-finite values.
Results may differ from a plain program's by a relative error of at most 0.001.
Values sent between devices are 32-bit elements; how exact they have to be, the bound alone decides.
A program may use at most 256 MiB of HBM per device.

v0:
```python
import math
import jax
import jax.numpy as jnp
from jax import lax
from jax.sharding import PartitionSpec as P

step_size = 0.25


def extended(block, sides, width):
    for axis, dim in sides:
        count = lax.axis_size(axis)
        forward = [(i, i + 1) for i in range(count - 1)]
        forward.append((count - 1, 0))
        backward = [(target, source) for source, target in forward]
        low = lax.ppermute(
            lax.slice_in_dim(block, block.shape[dim] - width, None, axis=dim), axis, forward
        )
        high = lax.ppermute(lax.slice_in_dim(block, 0, width, axis=dim), axis, backward)
        block = jnp.concatenate([low, block, high], axis=dim)
    return block


def upper_factor(gram):
    order = gram.shape[0]
    positions = jnp.arange(order)
    factor = jnp.zeros_like(gram)
    for column_index in range(order):
        above = factor[:, column_index]
        remainder = gram[column_index] - jnp.dot(
            above, factor, precision=lax.Precision.HIGHEST, preferred_element_type=jnp.float32
        )
        pivot = jnp.sqrt(remainder[column_index])
        new_row = jnp.where(positions >= column_index, remainder / pivot, 0.0)
        factor = factor.at[column_index].set(new_row)
    return factor


def upper_solve(factor, right_hand):
    order = factor.shape[0]
    solved = jnp.zeros_like(right_hand)
    for row_index in range(order - 1, -1, -1):
        partial_sum = jnp.dot(
            factor[row_index],
            solved,
            precision=lax.Precision.HIGHEST,
            preferred_element_type=jnp.float32,
        )
        solved = solved.at[row_index].set(
            (right_hand[row_index] - partial_sum) / factor[row_index, row_index]
        )
    return solved


def advance(padded, viscosity):
    centre = padded[:, 1:-1, 1:-1, :]
    forward_x = padded[:, 2:, 1:-1, :]
    backward_x = padded[:, :-2, 1:-1, :]
    forward_z = padded[:, 1:-1, 2:, :]
    backward_z = padded[:, 1:-1, :-2, :]
    walled = jnp.pad(centre, ((0, 0), (0, 0), (0, 0), (1, 1)))
    above_y = walled[..., 2:]
    below_y = walled[..., :-2]
    laplace = forward_x + backward_x + forward_z + backward_z + above_y + below_y - 6.0 * centre
    carried = (
        centre[0:1] * (forward_x - backward_x)
        + centre[1:2] * (above_y - below_y)
        + centre[2:3] * (forward_z - backward_z)
    )
    return centre + step_size * (viscosity * laplace - 0.5 * carried)


def shards(velocity, viscosity, basis, sigma, rotation):
    current = velocity
    history = [velocity]
    for repeat in range(2):
        padded = extended(current, (("slab", 1), ("tile", 2)), 1)
        current = advance(padded, viscosity)
        history.append(current)
    snapshots = lax.all_to_all(jnp.stack(history), "tile", split_axis=2, concat_axis=3, tiled=True)
    strip_width = basis.shape[2]
    row_count = (
        3
        * strip_width
        * lax.axis_size("slab")
        * lax.axis_size("tile")
        * basis.shape[3]
        * basis.shape[4]
    )
    row_scale = math.sqrt(row_count)
    width_all = sigma.shape[0] + 3
    scaled = basis.astype(jnp.float32) * sigma[:, None, None, None, None]
    columns = jnp.concatenate([scaled, snapshots], 0).reshape(width_all, -1)
    local_gram = jnp.dot(
        columns, columns.T, precision=lax.Precision.HIGHEST, preferred_element_type=jnp.float32
    )
    gram = lax.psum(local_gram, ("slab", "tile"))
    factor = upper_factor(gram)
    mixing = upper_solve(factor, rotation) * row_scale
    rotated = jnp.dot(
        mixing.T, columns, precision=lax.Precision.HIGHEST, preferred_element_type=jnp.float32
    )
    rotated = rotated.reshape(basis.shape).astype(jnp.bfloat16)
    return (current, factor / row_scale, rotated)


def solution(mesh):
    in_specs = (
        P(None, "slab", "tile", None),
        P("slab", "tile", None),
        P(None, None, ("slab", "tile"), None, None),
        P(),
        P(),
    )
    out_specs = (P(None, "slab", "tile", None), P(), P(None, None, ("slab", "tile"), None, None))
    return jax.shard_map(shards, mesh=mesh, in_specs=in_specs, out_specs=out_specs, check_vma=False)
```

profile of v0, /device:TPU:1, one launch (start us, length us, event | category | flops | bytes accessed | tf_op | source)
XLA Modules:
  0.0 461.0 jit_solution(1416673244914366114)
XLA Ops:
  1.4 4.3 collective-permute-start.1
  7.9 2.6 collective-permute-done
  10.5 3.9 collective-permute-start.2
  16.8 2.7 collective-permute-done.3
  19.6 1.8 multiply_add_fusion.1
  21.4 3.4 collective-permute-start.5
  25.7 4.1 collective-permute-done.4
  30.0 1.5 collective-permute-start.7
  32.9 2.2 collective-permute-done.7
  35.1 1.8 fusion.306
  36.9 1.6 pad_maximum_fusion.1
  38.6 3.8 all-to-all-start
  42.4 11.8 %convert_multiply_fusion = f32[32,3,4,128,128]{4,0,3,2,1:T(8,128)S(1)} fusion(bf16[32,3,4,128,128]{4,3,2,1,0:T(8,128)(2,1)} %param.147, f32[32]{0:T(128)} %param.148), kind=kLoop, calls=%fused_computation.8 | loop fusion | flops 12582912 | bytes 37748864 | tf_op jit(solution)/shard_map/mul | solution.py:92
  54.1 28.1 %copy.82 = f32[32,3,4,128,128]{4,3,2,1,0:T(8,128)} copy(f32[32,3,4,128,128]{4,0,3,2,1:T(8,128)S(1)} %convert_multiply_fusion) | data formatting | bytes 50331648 | tf_op jit(solution)/shard_map/mul | solution.py:92
  82.3 25.1 %copy.100 = f32[4,8,1536,128]{3,1,2,0:T(8,128)} copy(f32[4,8,1536,128]{3,2,1,0:T(8,128)} %bitcast.1128) | data formatting | bytes 50331648
  113.0 3.0 copy.46
  116.0 28.8 %fusion.9 = f32[35,35]{1,0:T(8,128)S(1)} fusion(f32[3,3,4,128,128]{4,0,3,2,1:T(4,128)S(1)} %bitcast.1130, f32[32,3,4,128,128]{4,0,3,2,1:T(8,128)} %copy-done.1), kind=kOutput, calls=%fused_computation.15 | convolution fusion | flops 2897018880 | bytes 27530020 | tf_op jit(solution)/shard_map/dot_general | solution.py:94
  144.8 68.9 %psum.7 = f32[35,35]{1,0:T(8,128)S(1)} all-reduce(f32[35,35]{1,0:T(8,128)S(1)} %fusion.9), channel_id=1, replica_groups=mesh['slab'=16,'tile'=8] {'slab','tile'}, use_global_device_ids=true, to_apply=%region_0.1 | all-reduce | flops 1225 | bytes 9800 | tf_op jit(solution)/shard_map/psum | solution.py:97
  299.7 1.5 fusion.89
  308.1 1.5 fusion.99
  313.2 1.5 fusion.105
  316.6 1.5 fusion.109
  323.3 1.5 fusion.117
  331.7 1.5 fusion.127
  333.4 1.5 fusion.129
  336.8 1.5 fusion.133
  345.3 1.5 fusion.143
  353.6 10.1 %pad_maximum_fusion = f32[35,196608]{1,0:T(8,128)S(1)} fusion(f32[3,196608]{1,0:T(4,128)S(1)} %bitcast.1131, f32[32,196608]{1,0:T(8,128)} %bitcast.1127), kind=kLoop, calls=%fused_computation.4 | loop fusion | flops 6881280 | bytes 55050240 | tf_op jit(solution)/shard_map/concatenate | solution.py:93
  363.7 14.4 %copy.89 = f32[5,8,1536,128]{3,2,1,0:T(8,128)} copy(f32[5,8,1536,128]{3,1,2,0:T(8,128)S(1)} %bitcast.1125) | data formatting | bytes 62914560
  378.1 20.3 %slice.2142 = f32[35,1536,128]{2,1,0:T(8,128)} slice(f32[40,1536,128]{2,1,0:T(8,128)} %bitcast.1126), slice={[0:35], [0:1536], [0:128]} | slice | bytes 55050240
  398.3 48.0 %fusion.6 = bf16[32,3,4,128,128]{4,0,3,2,1:T(8,128)(2,1)S(1)} fusion(f32[3,4,128,128,35]{3,2,1,0,4:T(8,128)} %bitcast.1124, f32[35,32]{0,1:T(8,128)S(1)} %scatter.349), kind=kOutput, calls=%fused_computation.9 | convolution fusion | flops 2648704000 | bytes 40112512 | tf_op jit(solution)/shard_map/dot_general | solution.py:100
  446.4 14.5 %copy.85 = bf16[32,3,4,128,128]{4,3,2,1,0:T(8,128)(2,1)} copy(bf16[32,3,4,128,128]{4,0,3,2,1:T(8,128)(2,1)S(1)} %fusion.6) | data formatting | bytes 25165824
  (368 shorter events, 115.3 us)
Async XLA Ops:
  1.4 5.3 %collective-permute-start.1 = (f32[3,1,16,128]{3,2,0,1:T(8,128)S(1)}, f32[3,1,16,128]{3,2,0,1:T(8,128)S(1)}, u32[]{:S(2)}, u32[]{:S(2)}) collective-permute-start(f32[3,1,16,128]{3,2,0,1:T(8,128)S(1)} %get-tuple-element.905), channel_id=1, source_target_pairs={{0,8},{8,16},{16,24},{24,32},{32,40},{40,48},{48,56},{56,64},{64,7... | collective-permute-start | bytes 73736 | tf_op jit(solution)/shard_map/ppermute | solution.py:16
  5.7 4.8 %collective-permute-start = (f32[3,1,16,128]{3,2,0,1:T(8,128)S(1)}, f32[3,1,16,128]{3,2,0,1:T(8,128)S(1)}, u32[]{:S(2)}, u32[]{:S(2)}) collective-permute-start(f32[3,1,16,128]{3,2,0,1:T(8,128)S(1)} %get-tuple-element.904), channel_id=1, source_target_pairs={{8,0},{16,8},{24,16},{32,24},{40,32},{48,40},{56,48},{64,56},{72,6... | collective-permute-start | bytes 73736 | tf_op jit(solution)/shard_map/ppermute | solution.py:19
  10.5 6.3 %collective-permute-start.2 = (f32[3,34,1,128]{3,2,0,1:T(1,128)S(1)}, f32[3,34,1,128]{3,2,0,1:T(1,128)S(1)}, u32[]{:S(2)}, u32[]{:S(2)}) collective-permute-start(f32[3,34,1,128]{3,2,0,1:T(1,128)S(1)} %get-tuple-element.892), channel_id=1, source_target_pairs={{1,0},{2,1},{3,2},{4,3},{5,4},{6,5},{7,6},{0,7},{9,8},{10,9},{11,1... | collective-permute-start | bytes 156680 | tf_op jit(solution)/shard_map/ppermute | solution.py:19
  14.5 5.1 %collective-permute-start.3 = (f32[3,34,1,128]{3,2,0,1:T(1,128)S(1)}, f32[3,34,1,128]{3,2,0,1:T(1,128)S(1)}, u32[]{:S(2)}, u32[]{:S(2)}) collective-permute-start(f32[3,34,1,128]{3,2,0,1:T(1,128)S(1)} %get-tuple-element.893), channel_id=1, source_target_pairs={{0,1},{1,2},{2,3},{3,4},{4,5},{5,6},{6,7},{7,0},{8,9},{9,10},{10,1... | collective-permute-start | bytes 156680 | tf_op jit(solution)/shard_map/ppermute | solution.py:16
  21.4 4.3 collective-permute-start.5
  24.8 5.1 %collective-permute-start.4 = (f32[3,1,16,128]{3,2,0,1:T(8,128)S(1)}, f32[3,1,16,128]{3,2,0,1:T(8,128)S(1)}, u32[]{:S(2)}, u32[]{:S(2)}) collective-permute-start(f32[3,1,16,128]{3,2,0,1:T(8,128)S(1)} %get-tuple-element.900), channel_id=1, source_target_pairs={{8,0},{16,8},{24,16},{32,24},{40,32},{48,40},{56,48},{64,56},{72,6... | collective-permute-start | bytes 73736 | tf_op jit(solution)/shard_map/ppermute | solution.py:19
  29.9 3.0 collective-permute-start.6
  30.0 5.2 %collective-permute-start.7 = (f32[3,34,1,128]{3,2,0,1:T(1,128)S(1)}, f32[3,34,1,128]{3,2,0,1:T(1,128)S(1)}, u32[]{:S(2)}, u32[]{:S(2)}) collective-permute-start(f32[3,34,1,128]{3,2,0,1:T(1,128)S(1)} %get-tuple-element.891), channel_id=1, source_target_pairs={{0,1},{1,2},{2,3},{3,4},{4,5},{5,6},{6,7},{7,0},{8,9},{9,10},{10,1... | collective-permute-start | bytes 156680 | tf_op jit(solution)/shard_map/ppermute | solution.py:16
  38.6 73.0 %all-to-all-start = ((f32[3,3,32,16,128]{4,3,1,0,2:T(8,128)}), f32[3,3,32,16,128]{4,3,1,0,2:T(8,128)S(1)}, u32[]{:S(2)}, u32[]{:S(2)}) async-start(f32[3,3,32,16,128]{4,3,1,0,2:T(8,128)} %pad_maximum_fusion.1), calls=%async_computation | async-start | bytes 4718592 | tf_op jit(solution)/shard_map/all_to_all | solution.py:80
  110.4 186.4 %copy-start.30 = (f32[32]{0:T(128)S(1)}, f32[32]{0:T(128)}, u32[]{:S(2)}) copy-start(f32[32]{0:T(128)} %get-tuple-element.888) | copy-start | bytes 388
  110.4 187.5 %copy-start.29 = (f32[32]{0:T(128)S(1)}, f32[32]{0:T(128)}, u32[]{:S(2)}) copy-start(f32[32]{0:T(128)} %get-tuple-element.887) | copy-start | bytes 388
  110.4 189.2 %copy-start.34 = (f32[32]{0:T(128)S(1)}, f32[32]{0:T(128)}, u32[]{:S(2)}) copy-start(f32[32]{0:T(128)} %get-tuple-element.886) | copy-start | bytes 388
  110.5 191.0 %copy-start.28 = (f32[32]{0:T(128)S(1)}, f32[32]{0:T(128)}, u32[]{:S(2)}) copy-start(f32[32]{0:T(128)} %get-tuple-element.885) | copy-start | bytes 388
  110.5 192.6 %copy-start.27 = (f32[32]{0:T(128)S(1)}, f32[32]{0:T(128)}, u32[]{:S(2)}) copy-start(f32[32]{0:T(128)} %get-tuple-element.884) | copy-start | bytes 388
  110.5 194.3 %copy-start.26 = (f32[32]{0:T(128)S(1)}, f32[32]{0:T(128)}, u32[]{:S(2)}) copy-start(f32[32]{0:T(128)} %get-tuple-element.883) | copy-start | bytes 388
  110.5 196.0 %copy-start.25 = (f32[32]{0:T(128)S(1)}, f32[32]{0:T(128)}, u32[]{:S(2)}) copy-start(f32[32]{0:T(128)} %get-tuple-element.882) | copy-start | bytes 388
  110.5 197.6 %copy-start.24 = (f32[32]{0:T(128)S(1)}, f32[32]{0:T(128)}, u32[]{:S(2)}) copy-start(f32[32]{0:T(128)} %get-tuple-element.881) | copy-start | bytes 388
  110.5 199.4 %copy-start.23 = (f32[32]{0:T(128)S(1)}, f32[32]{0:T(128)}, u32[]{:S(2)}) copy-start(f32[32]{0:T(128)} %get-tuple-element.880) | copy-start | bytes 388
  110.5 201.1 %copy-start.22 = (f32[32]{0:T(128)S(1)}, f32[32]{0:T(128)}, u32[]{:S(2)}) copy-start(f32[32]{0:T(128)} %get-tuple-element.879) | copy-start | bytes 388
  110.5 202.7 %copy-start.33 = (f32[32]{0:T(128)S(1)}, f32[32]{0:T(128)}, u32[]{:S(2)}) copy-start(f32[32]{0:T(128)} %get-tuple-element.878) | copy-start | bytes 388
  110.5 204.4 %copy-start.21 = (f32[32]{0:T(128)S(1)}, f32[32]{0:T(128)}, u32[]{:S(2)}) copy-start(f32[32]{0:T(128)} %get-tuple-element.877) | copy-start | bytes 388
  110.5 206.1 %copy-start.20 = (f32[32]{0:T(128)S(1)}, f32[32]{0:T(128)}, u32[]{:S(2)}) copy-start(f32[32]{0:T(128)} %get-tuple-element.876) | copy-start | bytes 388
  110.6 207.8 %copy-start.19 = (f32[32]{0:T(128)S(1)}, f32[32]{0:T(128)}, u32[]{:S(2)}) copy-start(f32[32]{0:T(128)} %get-tuple-element.875) | copy-start | bytes 388
  110.6 209.5 %copy-start.18 = (f32[32]{0:T(128)S(1)}, f32[32]{0:T(128)}, u32[]{:S(2)}) copy-start(f32[32]{0:T(128)} %get-tuple-element.873) | copy-start | bytes 388
  110.6 211.1 %copy-start.17 = (f32[32]{0:T(128)S(1)}, f32[32]{0:T(128)}, u32[]{:S(2)}) copy-start(f32[32]{0:T(128)} %get-tuple-element.872) | copy-start | bytes 388
  110.6 212.8 %copy-start.16 = (f32[32]{0:T(128)S(1)}, f32[32]{0:T(128)}, u32[]{:S(2)}) copy-start(f32[32]{0:T(128)} %get-tuple-element.871) | copy-start | bytes 388
  110.6 214.5 %copy-start.15 = (f32[32]{0:T(128)S(1)}, f32[32]{0:T(128)}, u32[]{:S(2)}) copy-start(f32[32]{0:T(128)} %get-tuple-element.870) | copy-start | bytes 388
  110.6 216.1 %copy-start.32 = (f32[32]{0:T(128)S(1)}, f32[32]{0:T(128)}, u32[]{:S(2)}) copy-start(f32[32]{0:T(128)} %get-tuple-element.869) | copy-start | bytes 388
  110.6 217.8 %copy-start.14 = (f32[32]{0:T(128)S(1)}, f32[32]{0:T(128)}, u32[]{:S(2)}) copy-start(f32[32]{0:T(128)} %get-tuple-element.868) | copy-start | bytes 388
  110.6 219.4 %copy-start.13 = (f32[32]{0:T(128)S(1)}, f32[32]{0:T(128)}, u32[]{:S(2)}) copy-start(f32[32]{0:T(128)} %get-tuple-element.867) | copy-start | bytes 388
  110.6 221.0 %copy-start.12 = (f32[32]{0:T(128)S(1)}, f32[32]{0:T(128)}, u32[]{:S(2)}) copy-start(f32[32]{0:T(128)} %get-tuple-element.866) | copy-start | bytes 388
  110.6 229.6 %copy-start.31 = (f32[32]{0:T(128)S(1)}, f32[32]{0:T(128)}, u32[]{:S(2)}) copy-start(f32[32]{0:T(128)} %get-tuple-element.861) | copy-start | bytes 388
  (13 other events, 372.9 us)
where the time goes:
time: 469 us; the launch traced here: 461 us
  local copies, waits for them, and re-layouts  153 us (33%)
  matrix products  153 us (33%)
  blocking collectives  68.9 us (15%)
  other arithmetic  28.8 us (6%)
  between operations  25.7 us (5%)
  starting transfers between devices  16.9 us (4%)
  waiting for transfers between devices  14.9 us (3%)
    unnamed x79, local copies, waits for them, and re-layouts  77.9 us
    psum x1, blocking collectives, shards(): gram = lax.psum(local_gram, ('slab', 'tile'))  68.9 us
    dot_general x35, matrix products, upper_solve(): jnp.dot(factor[row_index], solved, precision=lax.Precision.HIGHEST, prefe...  48.9 us
    dot_general x1, matrix products, shards(): jnp.dot(mixing.T, columns, precision=lax.Precision.HIGHEST, preferred_ele...  48 us
    dot_general x1, matrix products, shards(): jnp.dot(columns, columns.T, precision=lax.Precision.HIGHEST, preferred_el...  28.8 us
    mul x1, local copies, waits for them, and re-layouts, shards(): scaled = basis.astype(jnp.float32) * sigma[:, None, None, None, None]  28.1 us
    dot_general x35, matrix products, upper_factor(): jnp.dot(above, factor, precision=lax.Precision.HIGHEST, preferred_element...  27.4 us
    slice x34, local copies, waits for them, and re-layouts, upper_factor(): pivot = jnp.sqrt(remainder[column_index])  20.3 us
  transfers between devices with their start and end apart: 9, of which 7 were waited for; matrix products, arithmetic and copies ran while one was open for 16% of the time, Pallas kernels for 0%

commit v1 on v0

--- a/solution.py
+++ b/solution.py
@@ -94,7 +94,7 @@
     local_gram = jnp.dot(
         columns, columns.T, precision=lax.Precision.HIGHEST, preferred_element_type=jnp.float32
     )
-    gram = lax.psum(local_gram, ("slab", "tile"))
+    gram = lax.psum(lax.psum(local_gram, "slab"), "tile")
     factor = upper_factor(gram)
     mixing = upper_solve(factor, rotation) * row_scale
     rotated = jnp.dot(

time: 469 us -> 504 us (1.075)
  the two profiles are of different devices: /device:TPU:1 before, /device:TPU:0 now
where the time goes in v1:
time: 504 us; the launch traced here: 496 us
  local copies, waits for them, and re-layouts  153 us (30%)
  matrix products  153 us (30%)
  blocking collectives  103 us (20%)
  other arithmetic  28.8 us (6%)
  between operations  25.7 us (5%)
  starting transfers between devices  21.9 us (4%)
  waiting for transfers between devices  11.3 us (2%)
    psum x2, blocking collectives, shards(): gram = lax.psum(lax.psum(local_gram, 'slab'), 'tile')  103 us
    unnamed x79, local copies, waits for them, and re-layouts  77.9 us
    dot_general x35, matrix products, upper_solve(): jnp.dot(factor[row_index], solved, precision=lax.Precision.HIGHEST, prefe...  48.9 us
    dot_general x1, matrix products, shards(): jnp.dot(mixing.T, columns, precision=lax.Precision.HIGHEST, preferred_ele...  48 us
    dot_general x1, matrix products, shards(): jnp.dot(columns, columns.T, precision=lax.Precision.HIGHEST, preferred_el...  28.8 us
    mul x1, local copies, waits for them, and re-layouts, shards(): scaled = basis.astype(jnp.float32) * sigma[:, None, None, None, None]  28.1 us
    dot_general x35, matrix products, upper_factor(): jnp.dot(above, factor, precision=lax.Precision.HIGHEST, preferred_element...  27.4 us
    slice x34, local copies, waits for them, and re-layouts, upper_factor(): pivot = jnp.sqrt(remainder[column_index])  20.3 us
  transfers between devices with their start and end apart: 9, of which 5 were waited for; matrix products, arithmetic and copies ran while one was open for 15% of the time, Pallas kernels for 0%

profile of v1, /device:TPU:0, one launch (start us, length us, event | category | flops | bytes accessed | tf_op | source)
XLA Modules:
  0.0 496.5 jit_solution(1525343708568476188)
XLA Ops:
  1.4 5.4 %collective-permute-start = (f32[3,1,16,128]{3,2,0,1:T(8,128)S(1)}, f32[3,1,16,128]{3,2,0,1:T(8,128)S(1)}, u32[]{:S(2)}, u32[]{:S(2)}) collective-permute-start(f32[3,1,16,128]{3,2,0,1:T(8,128)S(1)} %get-tuple-element.904), channel_id=1, source_target_pairs={{8,0},{16,8},{24,16},{32,24},{40,32},{48,40},{56,48},{64,56},{72,6... | collective-permute-start | bytes 73736 | tf_op jit(solution)/shard_map/ppermute | solution.py:19
  6.8 1.5 collective-permute-done.1
  9.6 5.2 %collective-permute-start.2 = (f32[3,34,1,128]{3,2,0,1:T(1,128)S(1)}, f32[3,34,1,128]{3,2,0,1:T(1,128)S(1)}, u32[]{:S(2)}, u32[]{:S(2)}) collective-permute-start(f32[3,34,1,128]{3,2,0,1:T(1,128)S(1)} %get-tuple-element.892), channel_id=1, source_target_pairs={{1,0},{2,1},{3,2},{4,3},{5,4},{6,5},{7,6},{0,7},{9,8},{10,9},{11,1... | collective-permute-start | bytes 156680 | tf_op jit(solution)/shard_map/ppermute | solution.py:19
  17.2 3.9 collective-permute-done.3
  21.0 1.8 multiply_add_fusion.1
  23.0 5.3 %collective-permute-start.4 = (f32[3,1,16,128]{3,2,0,1:T(8,128)S(1)}, f32[3,1,16,128]{3,2,0,1:T(8,128)S(1)}, u32[]{:S(2)}, u32[]{:S(2)}) collective-permute-start(f32[3,1,16,128]{3,2,0,1:T(8,128)S(1)} %get-tuple-element.900), channel_id=1, source_target_pairs={{8,0},{16,8},{24,16},{32,24},{40,32},{48,40},{56,48},{64,56},{72,6... | collective-permute-start | bytes 73736 | tf_op jit(solution)/shard_map/ppermute | solution.py:19
  28.3 1.5 collective-permute-done.5
  30.3 1.7 collective-permute-start.7
  32.1 2.0 collective-permute-done.6
  34.1 2.4 collective-permute-done.7
  36.5 1.8 fusion.306
  38.3 1.6 pad_maximum_fusion.1
  39.9 3.8 all-to-all-start
  43.7 11.8 %convert_multiply_fusion = f32[32,3,4,128,128]{4,0,3,2,1:T(8,128)S(1)} fusion(bf16[32,3,4,128,128]{4,3,2,1,0:T(8,128)(2,1)} %param.147, f32[32]{0:T(128)} %param.148), kind=kLoop, calls=%fused_computation.8 | loop fusion | flops 12582912 | bytes 37748864 | tf_op jit(solution)/shard_map/mul | solution.py:92
  55.5 28.1 %copy.82 = f32[32,3,4,128,128]{4,3,2,1,0:T(8,128)} copy(f32[32,3,4,128,128]{4,0,3,2,1:T(8,128)S(1)} %convert_multiply_fusion) | data formatting | bytes 50331648 | tf_op jit(solution)/shard_map/mul | solution.py:92
  83.7 25.1 %copy.100 = f32[4,8,1536,128]{3,1,2,0:T(8,128)} copy(f32[4,8,1536,128]{3,2,1,0:T(8,128)} %bitcast.1128) | data formatting | bytes 50331648
  114.4 3.0 copy.46
  117.4 28.8 %fusion.9 = f32[35,35]{1,0:T(8,128)S(1)} fusion(f32[3,3,4,128,128]{4,0,3,2,1:T(4,128)S(1)} %bitcast.1130, f32[32,3,4,128,128]{4,0,3,2,1:T(8,128)} %copy-done.1), kind=kOutput, calls=%fused_computation.15 | convolution fusion | flops 2897018880 | bytes 27530020 | tf_op jit(solution)/shard_map/dot_general | solution.py:94
  146.2 69.3 %psum.14 = f32[35,35]{1,0:T(8,128)S(1)} all-reduce(f32[35,35]{1,0:T(8,128)S(1)} %fusion.9), channel_id=1, replica_groups=mesh['slab'=16,'tile'=8] {'slab'}, use_global_device_ids=true, to_apply=%region_0.1 | all-reduce | flops 1225 | bytes 9800 | tf_op jit(solution)/shard_map/psum | solution.py:97
  215.5 33.7 %psum.15 = f32[35,35]{1,0:T(8,128)S(1)} all-reduce(f32[35,35]{1,0:T(8,128)S(1)} %psum.14), channel_id=1, replica_groups=mesh['slab'=16,'tile'=8] {'tile'}, use_global_device_ids=true, to_apply=%region_1.2 | all-reduce | flops 1225 | bytes 9800 | tf_op jit(solution)/shard_map/psum | solution.py:97
  335.1 1.5 fusion.89
  343.6 1.5 fusion.99
  348.7 1.5 fusion.105
  367.1 1.5 fusion.127
  368.8 1.5 fusion.129
  372.3 1.5 fusion.133
  380.7 1.5 fusion.143
  389.0 10.1 %pad_maximum_fusion = f32[35,196608]{1,0:T(8,128)S(1)} fusion(f32[3,196608]{1,0:T(4,128)S(1)} %bitcast.1131, f32[32,196608]{1,0:T(8,128)} %bitcast.1127), kind=kLoop, calls=%fused_computation.4 | loop fusion | flops 6881280 | bytes 55050240 | tf_op jit(solution)/shard_map/concatenate | solution.py:93
  399.1 14.4 %copy.89 = f32[5,8,1536,128]{3,2,1,0:T(8,128)} copy(f32[5,8,1536,128]{3,1,2,0:T(8,128)S(1)} %bitcast.1125) | data formatting | bytes 62914560
  413.5 20.3 %slice.2142 = f32[35,1536,128]{2,1,0:T(8,128)} slice(f32[40,1536,128]{2,1,0:T(8,128)} %bitcast.1126), slice={[0:35], [0:1536], [0:128]} | slice | bytes 55050240
  433.8 48.0 %fusion.6 = bf16[32,3,4,128,128]{4,0,3,2,1:T(8,128)(2,1)S(1)} fusion(f32[3,4,128,128,35]{3,2,1,0,4:T(8,128)} %bitcast.1124, f32[35,32]{0,1:T(8,128)S(1)} %scatter.349), kind=kOutput, calls=%fused_computation.9 | convolution fusion | flops 2648704000 | bytes 40112512 | tf_op jit(solution)/shard_map/dot_general | solution.py:100
  481.8 14.5 %copy.85 = bf16[32,3,4,128,128]{4,3,2,1,0:T(8,128)(2,1)} copy(bf16[32,3,4,128,128]{4,0,3,2,1:T(8,128)(2,1)S(1)} %fusion.6) | data formatting | bytes 25165824
  (369 shorter events, 115.2 us)
Async XLA Ops:
  1.4 6.9 %collective-permute-start.1 = (f32[3,1,16,128]{3,2,0,1:T(8,128)S(1)}, f32[3,1,16,128]{3,2,0,1:T(8,128)S(1)}, u32[]{:S(2)}, u32[]{:S(2)}) collective-permute-start(f32[3,1,16,128]{3,2,0,1:T(8,128)S(1)} %get-tuple-element.905), channel_id=1, source_target_pairs={{0,8},{8,16},{16,24},{24,32},{32,40},{40,48},{48,56},{56,64},{64,7... | collective-permute-start | bytes 73736 | tf_op jit(solution)/shard_map/ppermute | solution.py:16
  1.4 8.1 %collective-permute-start = (f32[3,1,16,128]{3,2,0,1:T(8,128)S(1)}, f32[3,1,16,128]{3,2,0,1:T(8,128)S(1)}, u32[]{:S(2)}, u32[]{:S(2)}) collective-permute-start(f32[3,1,16,128]{3,2,0,1:T(8,128)S(1)} %get-tuple-element.904), channel_id=1, source_target_pairs={{8,0},{16,8},{24,16},{32,24},{40,32},{48,40},{56,48},{64,56},{72,6... | collective-permute-start | bytes 73736 | tf_op jit(solution)/shard_map/ppermute | solution.py:19
  9.6 7.6 %collective-permute-start.2 = (f32[3,34,1,128]{3,2,0,1:T(1,128)S(1)}, f32[3,34,1,128]{3,2,0,1:T(1,128)S(1)}, u32[]{:S(2)}, u32[]{:S(2)}) collective-permute-start(f32[3,34,1,128]{3,2,0,1:T(1,128)S(1)} %get-tuple-element.892), channel_id=1, source_target_pairs={{1,0},{2,1},{3,2},{4,3},{5,4},{6,5},{7,6},{0,7},{9,8},{10,9},{11,1... | collective-permute-start | bytes 156680 | tf_op jit(solution)/shard_map/ppermute | solution.py:19
  14.8 6.2 %collective-permute-start.3 = (f32[3,34,1,128]{3,2,0,1:T(1,128)S(1)}, f32[3,34,1,128]{3,2,0,1:T(1,128)S(1)}, u32[]{:S(2)}, u32[]{:S(2)}) collective-permute-start(f32[3,34,1,128]{3,2,0,1:T(1,128)S(1)} %get-tuple-element.893), channel_id=1, source_target_pairs={{0,1},{1,2},{2,3},{3,4},{4,5},{5,6},{6,7},{7,0},{8,9},{9,10},{10,1... | collective-permute-start | bytes 156680 | tf_op jit(solution)/shard_map/ppermute | solution.py:16
  22.9 6.9 %collective-permute-start.5 = (f32[3,1,16,128]{3,2,0,1:T(8,128)S(1)}, f32[3,1,16,128]{3,2,0,1:T(8,128)S(1)}, u32[]{:S(2)}, u32[]{:S(2)}) collective-permute-start(f32[3,1,16,128]{3,2,0,1:T(8,128)S(1)} %get-tuple-element.899), channel_id=1, source_target_pairs={{0,8},{8,16},{16,24},{24,32},{32,40},{40,48},{48,56},{56,64},{64,7... | collective-permute-start | bytes 73736 | tf_op jit(solution)/shard_map/ppermute | solution.py:16
  23.0 6.9 %collective-permute-start.4 = (f32[3,1,16,128]{3,2,0,1:T(8,128)S(1)}, f32[3,1,16,128]{3,2,0,1:T(8,128)S(1)}, u32[]{:S(2)}, u32[]{:S(2)}) collective-permute-start(f32[3,1,16,128]{3,2,0,1:T(8,128)S(1)} %get-tuple-element.900), channel_id=1, source_target_pairs={{8,0},{16,8},{24,16},{32,24},{40,32},{48,40},{56,48},{64,56},{72,6... | collective-permute-start | bytes 73736 | tf_op jit(solution)/shard_map/ppermute | solution.py:19
  29.9 4.2 collective-permute-start.6
  30.3 6.2 %collective-permute-start.7 = (f32[3,34,1,128]{3,2,0,1:T(1,128)S(1)}, f32[3,34,1,128]{3,2,0,1:T(1,128)S(1)}, u32[]{:S(2)}, u32[]{:S(2)}) collective-permute-start(f32[3,34,1,128]{3,2,0,1:T(1,128)S(1)} %get-tuple-element.891), channel_id=1, source_target_pairs={{0,1},{1,2},{2,3},{3,4},{4,5},{5,6},{6,7},{7,0},{8,9},{9,10},{10,1... | collective-permute-start | bytes 156680 | tf_op jit(solution)/shard_map/ppermute | solution.py:16
  39.9 73.0 %all-to-all-start = ((f32[3,3,32,16,128]{4,3,1,0,2:T(8,128)}), f32[3,3,32,16,128]{4,3,1,0,2:T(8,128)S(1)}, u32[]{:S(2)}, u32[]{:S(2)}) async-start(f32[3,3,32,16,128]{4,3,1,0,2:T(8,128)} %pad_maximum_fusion.1), calls=%async_computation | async-start | bytes 4718592 | tf_op jit(solution)/shard_map/all_to_all | solution.py:80
  111.8 220.1 %copy-start.30 = (f32[32]{0:T(128)S(1)}, f32[32]{0:T(128)}, u32[]{:S(2)}) copy-start(f32[32]{0:T(128)} %get-tuple-element.888) | copy-start | bytes 388
  111.8 221.6 %copy-start.29 = (f32[32]{0:T(128)S(1)}, f32[32]{0:T(128)}, u32[]{:S(2)}) copy-start(f32[32]{0:T(128)} %get-tuple-element.887) | copy-start | bytes 388
  111.8 223.3 %copy-start.34 = (f32[32]{0:T(128)S(1)}, f32[32]{0:T(128)}, u32[]{:S(2)}) copy-start(f32[32]{0:T(128)} %get-tuple-element.886) | copy-start | bytes 388
  111.8 225.0 %copy-start.28 = (f32[32]{0:T(128)S(1)}, f32[32]{0:T(128)}, u32[]{:S(2)}) copy-start(f32[32]{0:T(128)} %get-tuple-element.885) | copy-start | bytes 388
  111.8 226.6 %copy-start.27 = (f32[32]{0:T(128)S(1)}, f32[32]{0:T(128)}, u32[]{:S(2)}) copy-start(f32[32]{0:T(128)} %get-tuple-element.884) | copy-start | bytes 388
  111.8 228.3 %copy-start.26 = (f32[32]{0:T(128)S(1)}, f32[32]{0:T(128)}, u32[]{:S(2)}) copy-start(f32[32]{0:T(128)} %get-tuple-element.883) | copy-start | bytes 388
  111.8 230.0 %copy-start.25 = (f32[32]{0:T(128)S(1)}, f32[32]{0:T(128)}, u32[]{:S(2)}) copy-start(f32[32]{0:T(128)} %get-tuple-element.882) | copy-start | bytes 388
  111.8 231.7 %copy-start.24 = (f32[32]{0:T(128)S(1)}, f32[32]{0:T(128)}, u32[]{:S(2)}) copy-start(f32[32]{0:T(128)} %get-tuple-element.881) | copy-start | bytes 388
  111.9 233.5 %copy-start.23 = (f32[32]{0:T(128)S(1)}, f32[32]{0:T(128)}, u32[]{:S(2)}) copy-start(f32[32]{0:T(128)} %get-tuple-element.880) | copy-start | bytes 388
  111.9 235.1 %copy-start.22 = (f32[32]{0:T(128)S(1)}, f32[32]{0:T(128)}, u32[]{:S(2)}) copy-start(f32[32]{0:T(128)} %get-tuple-element.879) | copy-start | bytes 388
  111.9 236.8 %copy-start.33 = (f32[32]{0:T(128)S(1)}, f32[32]{0:T(128)}, u32[]{:S(2)}) copy-start(f32[32]{0:T(128)} %get-tuple-element.878) | copy-start | bytes 388
  111.9 238.5 %copy-start.21 = (f32[32]{0:T(128)S(1)}, f32[32]{0:T(128)}, u32[]{:S(2)}) copy-start(f32[32]{0:T(128)} %get-tuple-element.877) | copy-start | bytes 388
  111.9 240.1 %copy-start.20 = (f32[32]{0:T(128)S(1)}, f32[32]{0:T(128)}, u32[]{:S(2)}) copy-start(f32[32]{0:T(128)} %get-tuple-element.876) | copy-start | bytes 388
  111.9 241.8 %copy-start.19 = (f32[32]{0:T(128)S(1)}, f32[32]{0:T(128)}, u32[]{:S(2)}) copy-start(f32[32]{0:T(128)} %get-tuple-element.875) | copy-start | bytes 388
  111.9 243.5 %copy-start.18 = (f32[32]{0:T(128)S(1)}, f32[32]{0:T(128)}, u32[]{:S(2)}) copy-start(f32[32]{0:T(128)} %get-tuple-element.873) | copy-start | bytes 388
  111.9 245.2 %copy-start.17 = (f32[32]{0:T(128)S(1)}, f32[32]{0:T(128)}, u32[]{:S(2)}) copy-start(f32[32]{0:T(128)} %get-tuple-element.872) | copy-start | bytes 388
  111.9 246.8 %copy-start.16 = (f32[32]{0:T(128)S(1)}, f32[32]{0:T(128)}, u32[]{:S(2)}) copy-start(f32[32]{0:T(128)} %get-tuple-element.871) | copy-start | bytes 388
  111.9 248.5 %copy-start.15 = (f32[32]{0:T(128)S(1)}, f32[32]{0:T(128)}, u32[]{:S(2)}) copy-start(f32[32]{0:T(128)} %get-tuple-element.870) | copy-start | bytes 388
  112.0 250.2 %copy-start.32 = (f32[32]{0:T(128)S(1)}, f32[32]{0:T(128)}, u32[]{:S(2)}) copy-start(f32[32]{0:T(128)} %get-tuple-element.869) | copy-start | bytes 388
  112.0 251.8 %copy-start.14 = (f32[32]{0:T(128)S(1)}, f32[32]{0:T(128)}, u32[]{:S(2)}) copy-start(f32[32]{0:T(128)} %get-tuple-element.868) | copy-start | bytes 388
  112.0 253.5 %copy-start.13 = (f32[32]{0:T(128)S(1)}, f32[32]{0:T(128)}, u32[]{:S(2)}) copy-start(f32[32]{0:T(128)} %get-tuple-element.867) | copy-start | bytes 388
  112.0 255.1 %copy-start.12 = (f32[32]{0:T(128)S(1)}, f32[32]{0:T(128)}, u32[]{:S(2)}) copy-start(f32[32]{0:T(128)} %get-tuple-element.866) | copy-start | bytes 388
  112.0 263.7 %copy-start.31 = (f32[32]{0:T(128)S(1)}, f32[32]{0:T(128)}, u32[]{:S(2)}) copy-start(f32[32]{0:T(128)} %get-tuple-element.861) | copy-start | bytes 388
  (13 other events, 408.5 us)
